TPU v7x, 32 devices: a whole 2x2x4 slice. The times are simulated.
32 devices in a mesh: runs: 2 (over x), sec: 16 (over z, y, core).
Axes of the slice: x: 2, y: 2, z: 4, core: 2. Of those that a mesh axis runs over, the one named last changes fastest.
Arguments:
- edge_rows: bfloat16 [4096, 1024], P(('runs', 'sec')), parts along dimension 0, may hold values from -46 to 46
- corner: bfloat16 [32768, 1024], P(('runs', 'sec')), parts along dimension 0, may hold values from -1 to 2.2
- joining: int32 [32, 16], P('runs'), parts along dimension 0, may hold values from 0 to 15, as said below
- charge_left: int32 [4096], P(('runs', 'sec')), parts along dimension 0, may hold values from 0 to 15
- charge_right: int32 [4096], P(('runs', 'sec')), parts along dimension 0, may hold values from 0 to 15
Outputs:
- isometry: float32 [4096, 1024], P(('runs', 'sec')), parts along dimension 0
There are 2 independent parts, one for each index of `runs`. A program takes and returns all parts, laid end to end along the dimension named above; each array names one. Nothing has to cross between parts.
Inputs may be any that keep to these rules, and one draw needn't show every extreme that they name: joining[charge_left[e], charge_right[e]] names the block that row e needs; each row of joining names every block once; among the 128 rows of one device at most 16 need the same block, and one block, drawn per copy, receives exactly 16 rows from every device.
All inputs are finite; a program needn't handle non-finite values.
Results may differ from a plain program's by a relative error of at most 0.0003.
Values may be sent and summed in bfloat16 or wider, within the bound.
A program may use at most 128 MiB of HBM per device.

v0:
```python
import math
import jax
import jax.numpy as jnp
from jax import lax
from jax.sharding import PartitionSpec as P


def gram_of(images):
    return lax.dot_general(
        images, images, (((0,), (0,)), ((), ())), precision=lax.Precision.HIGHEST
    )


def reduce_gram(partial_gram):
    return lax.psum(partial_gram, "sec")


def solve_rows(gram_total, images, factor):
    lower = jnp.linalg.cholesky(gram_total)
    solved = lax.linalg.triangular_solve(
        lower, images, left_side=False, lower=True, transpose_a=True
    )
    return solved * factor


def per_device(edge_rows, corner, joining, charge_left, charge_right):
    row_count, feature_len = edge_rows.shape
    owners = lax.axis_size("sec")
    capacity = 2 * row_count // owners
    factor = math.sqrt(row_count * owners)
    target = joining[charge_left, charge_right]
    labels = jnp.arange(owners, dtype=jnp.int32)
    onehot = (target[:, None] == labels[None, :]).astype(jnp.int32)
    before = jnp.cumsum(onehot, axis=0) - onehot
    order_in = jnp.sum(before * onehot, axis=1)
    slot_index = target * capacity + order_in
    packed = (
        jnp.zeros((owners * capacity, feature_len), edge_rows.dtype).at[slot_index].set(edge_rows)
    )
    arrived = lax.all_to_all(
        packed.reshape(owners, capacity, feature_len),
        "sec",
        split_axis=0,
        concat_axis=0,
        tiled=True,
    )
    product = jnp.dot(
        arrived.reshape(owners * capacity, feature_len), corner, preferred_element_type=jnp.float32
    )
    returned = lax.all_to_all(
        product.reshape(owners, capacity, feature_len),
        "sec",
        split_axis=0,
        concat_axis=0,
        tiled=True,
    )
    home_rows = returned.reshape(owners * capacity, feature_len)[slot_index]
    gram_total = reduce_gram(gram_of(home_rows))
    result = solve_rows(gram_total, home_rows, factor)
    return result


def solution(mesh):
    placed = (
        P(("runs", "sec"), None),
        P(("runs", "sec"), None),
        P("runs", None),
        P(("runs", "sec")),
        P(("runs", "sec")),
    )
    return jax.shard_map(
        per_device, mesh=mesh, in_specs=placed, out_specs=P(("runs", "sec"), None), check_vma=False
    )
```

profile of v0, /device:TPU:0, one launch (start us, length us, event | category | flops | bytes accessed | tf_op | source)
XLA Modules:
  0.0 532.4 jit_solution(10985662273501543571)
XLA Ops:
  7.4 1.8 gather_fusion
  9.6 1.7 scatter_custom_fusion
  11.4 21.7 %all_to_all.10 = bf16[16,16,1024]{2,1,0:T(8,128)(2,1)S(1)} all-to-all(bf16[16,16,1024]{2,1,0:T(8,128)(2,1)S(1)} %bitcast.114), channel_id=1, replica_groups=mesh['runs'=2,'sec'=16] {'sec'}, dimensions={0} | all-to-all | bytes 1048576 | tf_op jit(solution)/shard_map/all_to_all | solution.py:40
  33.0 1.7 fusion.1
  34.7 4.1 all-to-all-start.1
  38.9 22.9 %all-to-all-done.1 = f32[16,16,1024]{2,1,0:T(8,128)S(1)} async-done(((f32[16,16,1024]{2,1,0:T(8,128)}), f32[16,16,1024]{2,1,0:T(8,128)S(1)}, u32[]{:S(2)}, u32[]{:S(2)}) %all-to-all-start.1) | async-done | bytes 1048608 | tf_op jit(solution)/shard_map/all_to_all | solution.py:50
  63.3 6.6 %fusion.73 = f32[1024,1024]{0,1:T(8,128)} fusion(f32[128,1024]{1,0:T(8,128)} %gather_fusion.1), kind=kOutput, calls=%fused_computation.176 | convolution fusion | flops 1610612736 | bytes 4718592 | tf_op jit(solution)/shard_map/dot_general | solution.py:9
  70.0 113.7 %all-reduce.3.cloned.1.call-done = f32[1024,1024]{0,1:T(8,128)} async-done(((f32[1024,1024]{0,1:T(8,128)}), f32[1024,1024]{0,1:T(8,128)}) %all-reduce.3.cloned.1.call-update) | async-done | bytes 4194320 | tf_op jit(solution)/shard_map/psum | solution.py:15
  183.8 5.8 %copy.10 = f32[1024,1024]{1,0:T(8,128)} copy(f32[1024,1024]{0,1:T(8,128)} %all-reduce.3.cloned.1.call-done) | data formatting | bytes 8388608 | tf_op jit(solution)/shard_map/psum | solution.py:15
  189.6 4.4 fusion
  194.0 1.9 copy-done.1
  195.9 11.7 %cholesky.223 = f32[128,128]{1,0:T(8,128)S(1)} custom-call(f32[128,128]{1,0:T(8,128)S(1)} %cholesky.580), custom_call_target="Cholesky" | custom-call | tf_op jit(solution)/shard_map/jit(cholesky)/cholesky | solution.py:19
  207.7 9.8 %custom-call.62 = f32[1,128,128]{1,2,0:T(8,128)S(1)} custom-call(f32[1,128,128]{2,1,0:T(8,128)S(1)} %get-tuple-element.69), custom_call_target="InvertDiagBlocksLowerTriangular" | custom-call | tf_op jit(solution)/shard_map/jit(cholesky)/cholesky | solution.py:19
  217.5 2.5 cholesky.255
  220.0 2.4 constant_dynamic-update-slice_fusion.31
  223.9 11.9 %cholesky.244 = f32[128,128]{1,0:T(8,128)S(1)} custom-call(f32[128,128]{1,0:T(8,128)S(1)} %cholesky.584), custom_call_target="Cholesky" | custom-call | tf_op jit(solution)/shard_map/jit(cholesky)/cholesky | solution.py:19
  236.4 9.8 %custom-call.63 = f32[1,128,128]{1,2,0:T(8,128)S(1)} custom-call(f32[1,128,128]{2,1,0:T(8,128)S(1)} %get-tuple-element.66), custom_call_target="InvertDiagBlocksLowerTriangular" | custom-call | tf_op jit(solution)/shard_map/jit(cholesky)/cholesky | solution.py:19
  247.5 2.1 convolution_subtract_fusion.1
  249.6 11.7 %cholesky.468 = f32[128,128]{1,0:T(8,128)S(1)} custom-call(f32[128,128]{1,0:T(8,128)S(1)} %cholesky.589), custom_call_target="Cholesky" | custom-call | tf_op jit(solution)/shard_map/jit(cholesky)/cholesky | solution.py:19
  262.6 9.8 %custom-call.64 = f32[1,128,128]{1,2,0:T(8,128)S(1)} custom-call(f32[1,128,128]{2,1,0:T(8,128)S(1)} %get-tuple-element.63), custom_call_target="InvertDiagBlocksLowerTriangular" | custom-call | tf_op jit(solution)/shard_map/jit(cholesky)/cholesky | solution.py:19
  273.6 2.3 convolution_subtract_fusion.2
  276.0 11.9 %cholesky.487 = f32[128,128]{1,0:T(8,128)S(1)} custom-call(f32[128,128]{1,0:T(8,128)S(1)} %cholesky.594), custom_call_target="Cholesky" | custom-call | tf_op jit(solution)/shard_map/jit(cholesky)/cholesky | solution.py:19
  289.2 9.8 %custom-call.65 = f32[1,128,128]{1,2,0:T(8,128)S(1)} custom-call(f32[1,128,128]{2,1,0:T(8,128)S(1)} %get-tuple-element.60), custom_call_target="InvertDiagBlocksLowerTriangular" | custom-call | tf_op jit(solution)/shard_map/jit(cholesky)/cholesky | solution.py:19
  300.1 2.3 convolution_subtract_fusion.3
  302.4 11.7 %cholesky.506 = f32[128,128]{1,0:T(8,128)S(1)} custom-call(f32[128,128]{1,0:T(8,128)S(1)} %cholesky.599), custom_call_target="Cholesky" | custom-call | tf_op jit(solution)/shard_map/jit(cholesky)/cholesky | solution.py:19
  315.4 10.2 %custom-call.66 = f32[1,128,128]{1,2,0:T(8,128)S(1)} custom-call(f32[1,128,128]{2,1,0:T(8,128)S(1)} %get-tuple-element.57), custom_call_target="InvertDiagBlocksLowerTriangular" | custom-call | tf_op jit(solution)/shard_map/jit(cholesky)/cholesky | solution.py:19
  326.6 2.3 convolution_subtract_fusion.4
  328.9 11.7 %cholesky.526 = f32[128,128]{1,0:T(8,128)S(1)} custom-call(f32[128,128]{1,0:T(8,128)S(1)} %cholesky.604), custom_call_target="Cholesky" | custom-call | tf_op jit(solution)/shard_map/jit(cholesky)/cholesky | solution.py:19
  341.9 9.8 %custom-call.67 = f32[1,128,128]{1,2,0:T(8,128)S(1)} custom-call(f32[1,128,128]{2,1,0:T(8,128)S(1)} %get-tuple-element.54), custom_call_target="InvertDiagBlocksLowerTriangular" | custom-call | tf_op jit(solution)/shard_map/jit(cholesky)/cholesky | solution.py:19
  352.7 2.0 convolution_subtract_fusion.5
  354.7 11.9 %cholesky.546 = f32[128,128]{1,0:T(8,128)S(1)} custom-call(f32[128,128]{1,0:T(8,128)S(1)} %cholesky.609), custom_call_target="Cholesky" | custom-call | tf_op jit(solution)/shard_map/jit(cholesky)/cholesky | solution.py:19
  367.9 9.8 %custom-call.68 = f32[1,128,128]{1,2,0:T(8,128)S(1)} custom-call(f32[1,128,128]{2,1,0:T(8,128)S(1)} %get-tuple-element.51), custom_call_target="InvertDiagBlocksLowerTriangular" | custom-call | tf_op jit(solution)/shard_map/jit(cholesky)/cholesky | solution.py:19
  378.5 1.8 convolution_subtract_fusion.11
  380.3 11.7 %cholesky.564 = f32[128,128]{1,0:T(8,128)S(1)} custom-call(f32[128,128]{1,0:T(8,128)S(1)} %convolution_subtract_fusion.11), custom_call_target="Cholesky" | custom-call | tf_op jit(solution)/shard_map/jit(cholesky)/cholesky | solution.py:19
  398.9 4.8 select_select_fusion
  403.8 27.6 %while.1 = (s32[]{:T(128)}, f32[1024,1024]{1,0:T(8,128)}, s32[8,2]{0,1:T(2,128)S(1)}, f32[8,128,128]{2,1,0:T(8,128)}, s32[]{:T(128)}) while((s32[]{:T(128)}, f32[1024,1024]{1,0:T(8,128)}, s32[8,2]{0,1:T(2,128)S(1)}, f32[8,128,128]{2,1,0:T(8,128)}, s32[]{:T(128)}) %tuple.57), condition=%wide.while_cond, body=%wide.while_body.sunk | while | flops 2 | bytes 132705 | solution.py:20
  404.4 2.9 bitcast_dynamic-update-slice_fusion.2
  407.9 2.8 bitcast_dynamic-update-slice_fusion.2
  411.3 2.8 bitcast_dynamic-update-slice_fusion.2
  414.8 2.8 bitcast_dynamic-update-slice_fusion.2
  418.3 2.8 bitcast_dynamic-update-slice_fusion.2
  421.7 2.8 bitcast_dynamic-update-slice_fusion.2
  425.2 2.8 bitcast_dynamic-update-slice_fusion.2
  428.7 2.8 bitcast_dynamic-update-slice_fusion.2
  431.4 79.6 %custom-call.69 = f32[8,128,128]{1,2,0:T(8,128)S(1)} custom-call(f32[8,128,128]{2,1,0:T(8,128)} %get-tuple-element.12), custom_call_target="InvertDiagBlocksLowerTriangular" | custom-call | tf_op jit(solution)/shard_map/triangular_solve | solution.py:20
  518.0 1.7 convolution_subtract_fusion.8
  519.9 1.8 convolution_subtract_fusion.7
  522.0 1.9 convolution_subtract_fusion.6
  (76 shorter events, 33.7 us)
Async XLA Ops:
  6.5 26.5 %copy-start = (bf16[1024,1024]{1,0:T(8,128)(2,1)S(1)}, bf16[1024,1024]{1,0:T(8,128)(2,1)}, u32[]{:S(2)}) copy-start(bf16[1024,1024]{1,0:T(8,128)(2,1)} %param.6) | copy-start | bytes 6291460
  34.7 27.0 %all-to-all-start.1 = ((f32[16,16,1024]{2,1,0:T(8,128)}), f32[16,16,1024]{2,1,0:T(8,128)S(1)}, u32[]{:S(2)}, u32[]{:S(2)}) async-start(f32[16,16,1024]{2,1,0:T(8,128)} %fusion.1), calls=%async_computation.1 | async-start | bytes 2097152 | tf_op jit(solution)/shard_map/all_to_all | solution.py:50
  38.8 144.9 %all-reduce.3.cloned.1.call-start = ((), (), s32[]{:S(2)}) async-start(), calls=%async_computation.2 | async-start | bytes 8388608 | tf_op jit(solution)/shard_map/psum | solution.py:15
  194.0 1.9 copy-start.1
  398.9 112.1 %copy-start.2 = (f32[128,1024]{1,0:T(8,128)S(1)}, f32[128,1024]{1,0:T(8,128)}, u32[]{:S(2)}) copy-start(f32[128,1024]{1,0:T(8,128)} %gather_fusion.1) | copy-start | bytes 1572868
Sparse Core Ops, SparseCore 0:
  70.1 113.5 all-reduce.2
where the time goes:
time: 539 us; the launch traced here: 532 us
  other arithmetic  263 us (49%)
  waiting for transfers between devices  137 us (25%)
  matrix products  44.5 us (8%)
  local copies, waits for them, and re-layouts  44 us (8%)
  blocking collectives  21.7 us (4%)
  between operations  18.9 us (4%)
    another operation x30, other arithmetic, solve_rows(): lower = jnp.linalg.cholesky(gram_total)  172 us
    psum x1, waiting for transfers between devices, reduce_gram(): return lax.psum(partial_gram, 'sec')  114 us
    another operation x3, other arithmetic, solve_rows(): lax.linalg.triangular_solve(lower, images, left_side=False, lower=True, t...  84.5 us
    another operation x24, local copies, waits for them, and re-layouts  27.6 us
    another operation x14, matrix products, solve_rows(): lower = jnp.linalg.cholesky(gram_total)  23.1 us
    all_to_all x1, waiting for transfers between devices, per_device(): lax.all_to_all(product.reshape(owners, capacity, feature_len), 'sec', spl...  22.9 us
    all_to_all x1, blocking collectives, per_device(): lax.all_to_all(packed.reshape(owners, capacity, feature_len), 'sec', spli...  21.7 us
    another operation x15, matrix products, solve_rows(): lax.linalg.triangular_solve(lower, images, left_side=False, lower=True, t...  13.1 us
  transfers between devices with their start and end apart: 2, of which 2 were waited for; matrix products, arithmetic and copies ran while one was open for 0% of the time, Pallas kernels for 0%

commit v1 on v0

--- a/solution.py
+++ b/solution.py
@@ -12,7 +12,7 @@
 
 
 def reduce_gram(partial_gram):
-    return lax.psum(partial_gram, "sec")
+    return jnp.sum(lax.all_gather(partial_gram, "sec"), axis=0)
 
 
 def solve_rows(gram_total, images, factor):

time: 539 us -> 777 us (1.44)
  waiting for transfers between devices: 137 us -> 351 us
  other arithmetic: 263 us -> 285 us
    all_gather x0 -> x1, waiting for transfers between devices: none -> 328 us  [reduce_gram(): return jnp.sum(lax.all_gather(partial_gram, 'sec'), axis=0)]
    psum x1 -> x0, waiting for transfers between devices: 114 us -> none  [reduce_gram(): return lax.psum(partial_gram, 'sec')]
    reduce_sum x0 -> x1, other arithmetic: none -> 22.9 us  [reduce_gram(): return jnp.sum(lax.all_gather(partial_gram, 'sec'), axis=0)]
where the time goes in v1:
time: 777 us; the launch traced here: 770 us
  waiting for transfers between devices  351 us (45%)
  other arithmetic  285 us (37%)
  matrix products  44.5 us (6%)
  local copies, waits for them, and re-layouts  44 us (6%)
  blocking collectives  21.7 us (3%)
  between operations  18.8 us (2%)
    all_gather x1, waiting for transfers between devices, reduce_gram(): return jnp.sum(lax.all_gather(partial_gram, 'sec'), axis=0)  328 us
    another operation x30, other arithmetic, solve_rows(): lower = jnp.linalg.cholesky(gram_total)  172 us
    another operation x3, other arithmetic, solve_rows(): lax.linalg.triangular_solve(lower, images, left_side=False, lower=True, t...  84.5 us
    another operation x24, local copies, waits for them, and re-layouts  27.6 us
    another operation x14, matrix products, solve_rows(): lower = jnp.linalg.cholesky(gram_total)  23.1 us
    reduce_sum x1, other arithmetic, reduce_gram(): return jnp.sum(lax.all_gather(partial_gram, 'sec'), axis=0)  22.9 us
    all_to_all x1, waiting for transfers between devices, per_device(): lax.all_to_all(product.reshape(owners, capacity, feature_len), 'sec', spl...  22.9 us
    all_to_all x1, blocking collectives, per_device(): lax.all_to_all(packed.reshape(owners, capacity, feature_len), 'sec', spli...  21.7 us
  transfers between devices with their start and end apart: 2, of which 2 were waited for; matrix products, arithmetic and copies ran while one was open for 0% of the time, Pallas kernels for 0%

profile of v1, /device:TPU:0, one launch (start us, length us, event | category | flops | bytes accessed | tf_op | source)
XLA Modules:
  0.0 769.9 jit_solution(12416424832293204199)
XLA Ops:
  7.4 1.8 gather_fusion
  9.6 1.7 scatter_custom_fusion
  11.4 21.7 %all_to_all.10 = bf16[16,16,1024]{2,1,0:T(8,128)(2,1)S(1)} all-to-all(bf16[16,16,1024]{2,1,0:T(8,128)(2,1)S(1)} %bitcast.115), channel_id=1, replica_groups=mesh['runs'=2,'sec'=16] {'sec'}, dimensions={0} | all-to-all | bytes 1048576 | tf_op jit(solution)/shard_map/all_to_all | solution.py:40
  33.0 1.7 fusion.1
  34.7 4.1 all-to-all-start.1
  38.9 22.9 %all-to-all-done.1 = f32[16,16,1024]{2,1,0:T(8,128)S(1)} async-done(((f32[16,16,1024]{2,1,0:T(8,128)}), f32[16,16,1024]{2,1,0:T(8,128)S(1)}, u32[]{:S(2)}, u32[]{:S(2)}) %all-to-all-start.1) | async-done | bytes 1048608 | tf_op jit(solution)/shard_map/all_to_all | solution.py:50
  63.3 6.6 fusion.73
  70.0 328.4 %all-gather.3.cloned.1.call-done = f32[16384,1024]{1,0:T(8,128)} async-done(((f32[1024,1024]{1,0:T(8,128)}), f32[16384,1024]{1,0:T(8,128)}) %all-gather.3.cloned.1.call-update) | async-done | bytes 67108880 | tf_op jit(solution)/shard_map/all_gather | solution.py:15
  398.4 22.9 %reduce_sum.19 = f32[1024,1024]{1,0:T(8,128)} reduce(f32[16,1024,1024]{2,1,0:T(8,128)} %bitcast.5, f32[]{:T(128)} %constant.278.clone.1), dimensions={0}, to_apply=%region_3.4 | reduce | flops 15728640 | bytes 71303168 | tf_op jit(solution)/shard_map/reduce_sum | solution.py:15
  421.4 5.8 copy.10
  427.2 4.4 fusion
  431.6 1.9 copy-done.1
  433.6 11.7 %cholesky.223 = f32[128,128]{1,0:T(8,128)S(1)} custom-call(f32[128,128]{1,0:T(8,128)S(1)} %cholesky.580), custom_call_target="Cholesky" | custom-call | tf_op jit(solution)/shard_map/jit(cholesky)/cholesky | solution.py:19
  445.3 2.5 cholesky.255
  447.8 9.8 %custom-call.62 = f32[1,128,128]{1,2,0:T(8,128)S(1)} custom-call(f32[1,128,128]{2,1,0:T(8,128)S(1)} %get-tuple-element.69), custom_call_target="InvertDiagBlocksLowerTriangular" | custom-call | tf_op jit(solution)/shard_map/jit(cholesky)/cholesky | solution.py:19
  457.6 2.4 constant_dynamic-update-slice_fusion.31
  461.6 11.9 %cholesky.244 = f32[128,128]{1,0:T(8,128)S(1)} custom-call(f32[128,128]{1,0:T(8,128)S(1)} %cholesky.584), custom_call_target="Cholesky" | custom-call | tf_op jit(solution)/shard_map/jit(cholesky)/cholesky | solution.py:19
  474.1 9.8 %custom-call.63 = f32[1,128,128]{1,2,0:T(8,128)S(1)} custom-call(f32[1,128,128]{2,1,0:T(8,128)S(1)} %get-tuple-element.66), custom_call_target="InvertDiagBlocksLowerTriangular" | custom-call | tf_op jit(solution)/shard_map/jit(cholesky)/cholesky | solution.py:19
  485.1 2.1 convolution_subtract_fusion.1
  487.2 11.7 %cholesky.468 = f32[128,128]{1,0:T(8,128)S(1)} custom-call(f32[128,128]{1,0:T(8,128)S(1)} %cholesky.589), custom_call_target="Cholesky" | custom-call | tf_op jit(solution)/shard_map/jit(cholesky)/cholesky | solution.py:19
  500.2 9.8 %custom-call.64 = f32[1,128,128]{1,2,0:T(8,128)S(1)} custom-call(f32[1,128,128]{2,1,0:T(8,128)S(1)} %get-tuple-element.63), custom_call_target="InvertDiagBlocksLowerTriangular" | custom-call | tf_op jit(solution)/shard_map/jit(cholesky)/cholesky | solution.py:19
  511.2 2.3 convolution_subtract_fusion.2
  513.5 11.9 %cholesky.487 = f32[128,128]{1,0:T(8,128)S(1)} custom-call(f32[128,128]{1,0:T(8,128)S(1)} %cholesky.594), custom_call_target="Cholesky" | custom-call | tf_op jit(solution)/shard_map/jit(cholesky)/cholesky | solution.py:19
  526.7 9.8 %custom-call.65 = f32[1,128,128]{1,2,0:T(8,128)S(1)} custom-call(f32[1,128,128]{2,1,0:T(8,128)S(1)} %get-tuple-element.60), custom_call_target="InvertDiagBlocksLowerTriangular" | custom-call | tf_op jit(solution)/shard_map/jit(cholesky)/cholesky | solution.py:19
  537.6 2.3 convolution_subtract_fusion.3
  540.0 11.7 %cholesky.506 = f32[128,128]{1,0:T(8,128)S(1)} custom-call(f32[128,128]{1,0:T(8,128)S(1)} %cholesky.599), custom_call_target="Cholesky" | custom-call | tf_op jit(solution)/shard_map/jit(cholesky)/cholesky | solution.py:19
  553.0 10.2 %custom-call.66 = f32[1,128,128]{1,2,0:T(8,128)S(1)} custom-call(f32[1,128,128]{2,1,0:T(8,128)S(1)} %get-tuple-element.57), custom_call_target="InvertDiagBlocksLowerTriangular" | custom-call | tf_op jit(solution)/shard_map/jit(cholesky)/cholesky | solution.py:19
  564.2 2.3 convolution_subtract_fusion.4
  566.5 11.7 %cholesky.526 = f32[128,128]{1,0:T(8,128)S(1)} custom-call(f32[128,128]{1,0:T(8,128)S(1)} %cholesky.604), custom_call_target="Cholesky" | custom-call | tf_op jit(solution)/shard_map/jit(cholesky)/cholesky | solution.py:19
  579.5 9.8 %custom-call.67 = f32[1,128,128]{1,2,0:T(8,128)S(1)} custom-call(f32[1,128,128]{2,1,0:T(8,128)S(1)} %get-tuple-element.54), custom_call_target="InvertDiagBlocksLowerTriangular" | custom-call | tf_op jit(solution)/shard_map/jit(cholesky)/cholesky | solution.py:19
  590.2 2.0 convolution_subtract_fusion.5
  592.3 11.9 %cholesky.546 = f32[128,128]{1,0:T(8,128)S(1)} custom-call(f32[128,128]{1,0:T(8,128)S(1)} %cholesky.609), custom_call_target="Cholesky" | custom-call | tf_op jit(solution)/shard_map/jit(cholesky)/cholesky | solution.py:19
  605.4 9.8 %custom-call.68 = f32[1,128,128]{1,2,0:T(8,128)S(1)} custom-call(f32[1,128,128]{2,1,0:T(8,128)S(1)} %get-tuple-element.51), custom_call_target="InvertDiagBlocksLowerTriangular" | custom-call | tf_op jit(solution)/shard_map/jit(cholesky)/cholesky | solution.py:19
  616.0 1.8 convolution_subtract_fusion.11
  617.8 11.7 %cholesky.564 = f32[128,128]{1,0:T(8,128)S(1)} custom-call(f32[128,128]{1,0:T(8,128)S(1)} %convolution_subtract_fusion.11), custom_call_target="Cholesky" | custom-call | tf_op jit(solution)/shard_map/jit(cholesky)/cholesky | solution.py:19
  636.4 4.8 select_select_fusion
  641.2 27.7 %while.1 = (s32[]{:T(128)}, f32[1024,1024]{1,0:T(8,128)}, s32[8,2]{0,1:T(2,128)S(1)}, f32[8,128,128]{2,1,0:T(8,128)}, s32[]{:T(128)}) while((s32[]{:T(128)}, f32[1024,1024]{1,0:T(8,128)}, s32[8,2]{0,1:T(2,128)S(1)}, f32[8,128,128]{2,1,0:T(8,128)}, s32[]{:T(128)}) %tuple.57), condition=%wide.while_cond, body=%wide.while_body.sunk | while | flops 2 | bytes 132705 | solution.py:20
  641.9 2.8 bitcast_dynamic-update-slice_fusion.2
  645.3 2.8 bitcast_dynamic-update-slice_fusion.2
  648.8 2.8 bitcast_dynamic-update-slice_fusion.2
  652.2 2.8 bitcast_dynamic-update-slice_fusion.2
  655.7 2.8 bitcast_dynamic-update-slice_fusion.2
  659.2 2.9 bitcast_dynamic-update-slice_fusion.2
  662.7 2.8 bitcast_dynamic-update-slice_fusion.2
  666.1 2.8 bitcast_dynamic-update-slice_fusion.2
  668.9 79.6 %custom-call.69 = f32[8,128,128]{1,2,0:T(8,128)S(1)} custom-call(f32[8,128,128]{2,1,0:T(8,128)} %get-tuple-element.12), custom_call_target="InvertDiagBlocksLowerTriangular" | custom-call | tf_op jit(solution)/shard_map/triangular_solve | solution.py:20
  757.4 1.8 convolution_subtract_fusion.7
  759.5 1.9 convolution_subtract_fusion.6
  (77 shorter events, 35.3 us)
Async XLA Ops:
  6.5 26.5 %copy-start = (bf16[1024,1024]{1,0:T(8,128)(2,1)S(1)}, bf16[1024,1024]{1,0:T(8,128)(2,1)}, u32[]{:S(2)}) copy-start(bf16[1024,1024]{1,0:T(8,128)(2,1)} %param.6) | copy-start | bytes 6291460
  34.7 27.0 %all-to-all-start.1 = ((f32[16,16,1024]{2,1,0:T(8,128)}), f32[16,16,1024]{2,1,0:T(8,128)S(1)}, u32[]{:S(2)}, u32[]{:S(2)}) async-start(f32[16,16,1024]{2,1,0:T(8,128)} %fusion.1), calls=%async_computation.1 | async-start | bytes 2097152 | tf_op jit(solution)/shard_map/all_to_all | solution.py:50
  38.8 359.6 %all-gather.3.cloned.1.call-start = ((), (), s32[]{:S(2)}) async-start(), calls=%async_computation.2 | async-start | bytes 71303168 | tf_op jit(solution)/shard_map/all_gather | solution.py:15
  431.6 1.9 copy-start.1
  636.4 112.1 %copy-start.2 = (f32[128,1024]{1,0:T(8,128)S(1)}, f32[128,1024]{1,0:T(8,128)}, u32[]{:S(2)}) copy-start(f32[128,1024]{1,0:T(8,128)} %gather_fusion.1) | copy-start | bytes 1572868
Sparse Core Ops, SparseCore 0:
  70.1 328.2 all-gather.2
